TPU v7x, 512 devices: a whole 4x4x16 slice. The times are simulated.
512 devices in a mesh: dp: 64 (over x, z), tensor: 8 (over y, core).
Axes of the slice: x: 4, y: 4, z: 16, core: 2. Of those that a mesh axis runs over, the one named last changes fastest.
Arguments:
- tokens: bfloat16 [8192, 8192], P('dp', 'tensor'), may hold values from -6 to 6
- hidden_grad: bfloat16 [8192, 28672], P('dp', 'tensor'), may hold values from -0.0625 to 0.0625
- masters: float32 [8, 64, 128, 128], P('tensor', 'dp'), may hold values from -0.5 to 0.5
- block_row: int32 [8, 32], P('tensor'), may hold values from 0 to 63, as said below
- block_col: int32 [8, 32], P('tensor'), may hold values from 0 to 27
- owners: int32 [8, 64], P('tensor'), may hold values from 0 to 63, as said below
Outputs:
- grads: float32 [8, 192, 128, 128], P('tensor', 'dp')
Inputs may be any that keep to these rules, and one draw needn't show every extreme that they name: `block_row`: in each slice the kept places are distinct. `owners`: in each slice every owner takes at most 3 of the 64 kept blocks, and some owner takes exactly 3.
All inputs are finite; a program needn't handle non-finite values.
Results may differ from a plain program's by a relative error of at most 0.0044.
Values may be sent and summed in bfloat16 or wider, within the bound.
A program may use at most 64 MiB of HBM per device.

v0:
```python
import jax
import jax.numpy as jnp
from jax import lax
from jax.sharding import PartitionSpec as P


def slot_index(owner_row, capacity):
    count_all = owner_row.shape[0]
    same_owner = owner_row[:, None] == owner_row[None, :]
    earlier = (
        jnp.arange(count_all, dtype=jnp.int32)[None, :]
        < jnp.arange(count_all, dtype=jnp.int32)[:, None]
    )
    rank_index = jnp.sum(
        jnp.logical_and(same_owner, earlier).astype(jnp.int32), axis=1, dtype=jnp.int32
    )
    return owner_row * capacity + rank_index


def column_total(part, same_column):
    return jnp.einsum("tjc,kj->tkc", part, same_column, precision=lax.Precision.HIGHEST)


def local(tokens, hidden_grad, masters, block_row, block_col, owners):
    high = lax.Precision.HIGHEST
    features = lax.all_gather(tokens, "tensor", axis=1, tiled=True)
    token_count = features.shape[0]
    block_side = masters.shape[-1]
    kept_count = block_row.shape[1]
    weights = lax.all_gather(masters.astype(jnp.bfloat16), "dp", axis=1, tiled=True)[0]
    row_index = block_row[0]
    column_index = block_col[0]
    by_block = features.reshape(token_count, features.shape[1] // block_side, block_side)
    selected = jnp.take(by_block, row_index, axis=1)
    gate_part = jnp.einsum(
        "tkb,kbc->tkc", selected, weights[:kept_count], preferred_element_type=jnp.float32
    )
    up_part = jnp.einsum(
        "tkb,kbc->tkc", selected, weights[kept_count:], preferred_element_type=jnp.float32
    )
    same_column = (column_index[:, None] == column_index[None, :]).astype(jnp.float32)
    gate_value = column_total(gate_part, same_column)
    up_value = column_total(up_part, same_column)
    grad_columns = hidden_grad.reshape(token_count, hidden_grad.shape[1] // block_side, block_side)
    upstream = jnp.take(grad_columns, column_index, axis=1).astype(jnp.float32)
    sigmoid_gate = jax.nn.sigmoid(gate_value)
    gate_grad = (
        upstream * up_value * sigmoid_gate * (1.0 + gate_value * (1.0 - sigmoid_gate))
    ).astype(jnp.bfloat16)
    up_grad = (upstream * gate_value * sigmoid_gate).astype(jnp.bfloat16)
    grad_gate = jnp.einsum("tkb,tkc->kbc", selected, gate_grad, preferred_element_type=jnp.float32)
    grad_up = jnp.einsum("tkb,tkc->kbc", selected, up_grad, preferred_element_type=jnp.float32)
    block_grads = jnp.concatenate([grad_gate, grad_up], axis=0)
    owner_count = lax.axis_size("dp")
    capacity = 3 * block_grads.shape[0] // owner_count
    slot_list = slot_index(owners[0], capacity)
    summed = lax.psum(block_grads, "dp")
    own_slots = lax.axis_index("dp") * capacity + jnp.arange(capacity, dtype=jnp.int32)
    selector = (own_slots[:, None] == slot_list[None, :]).astype(jnp.float32)
    result = jnp.einsum("sk,kbc->sbc", selector, summed, precision=high)
    return result[None]


def solution(mesh):
    return jax.shard_map(
        local,
        mesh=mesh,
        in_specs=(
            P("dp", "tensor"),
            P("dp", "tensor"),
            P("tensor", "dp", None, None),
            P("tensor", None),
            P("tensor", None),
            P("tensor", None),
        ),
        out_specs=P("tensor", "dp", None, None),
        check_vma=False,
    )
```

profile of v0, /device:TPU:8, one launch (start us, length us, event | category | flops | bytes accessed | tf_op | source)
XLA Modules:
  0.0 505.0 jit_solution(9367897133489525281)
XLA Ops:
  6.5 0.0 all-gather.3.cloned.1.call-start
  6.5 1.8 copy.48
  8.3 0.0 copy-start.3
  8.3 0.0 all-gather.3.cloned.1.call-update
  8.4 0.0 all-gather.5.cloned.1.call-start
  8.4 1.5 bitcast_convert_fusion
  9.9 0.0 all-gather.5.cloned.1.call-update
  9.9 0.0 all-reduce.2.cloned.1.call-start
  10.0 1.6 copy.51
  11.5 0.0 copy-start.2
  11.5 0.6 copy.52
  12.2 0.0 copy-done.3
  12.2 1.6 gather_fusion.1
  13.9 0.0 copy-done.2
  13.9 31.9 %all-gather.3.cloned.1.call-done = bf16[128,8192]{0,1:T(8,128)(2,1)} async-done(((bf16[128,1024]{0,1:T(8,128)(2,1)}), bf16[128,8192]{0,1:T(8,128)(2,1)}) %all-gather.3.cloned.1.call-update) | async-done | bytes 2097168 | tf_op jit(solution)/shard_map/all_gather | solution.py:26
  45.8 3.2 copy.49
  49.1 0.7 gather_fusion
  49.8 0.6 fusion.24
  50.5 1.2 copy.61
  51.7 139.4 %all-gather.5.cloned.1.call-done = bf16[1,64,128,128]{3,2,0,1:T(8,128)(2,1)} async-done(((bf16[1,1,128,128]{3,2,0,1:T(8,128)(2,1)}), bf16[1,64,128,128]{3,2,0,1:T(8,128)(2,1)}) %all-gather.5.cloned.1.call-update) | async-done | bytes 2097168 | tf_op jit(solution)/shard_map/all_gather | solution.py:30
  191.0 0.0 copy-start
  191.0 1.9 convolution_bitcast_fusion
  192.9 0.0 copy-done
  192.9 0.0 copy-start.1
  193.0 0.5 convolution_bitcast_fusion.1
  193.5 0.7 copy-done.1
  194.2 3.5 fusion.9
  197.7 3.8 fusion.7
  201.5 0.8 fusion.22
  202.2 0.8 fusion.20
  203.0 2.5 pad_maximum_fusion
  205.5 0.0 copy-start.4
  205.5 0.0 all-reduce.2.cloned.1.call-update
  205.5 0.6 copy-done.4
  206.1 0.2 convert_reduce_fusion
  206.3 285.7 %all-reduce.2.cloned.1.call-done = f32[64,128,128]{2,1,0:T(8,128)} async-done(((f32[64,128,128]{2,1,0:T(8,128)}), f32[64,128,128]{2,1,0:T(8,128)}) %all-reduce.2.cloned.1.call-update) | async-done | bytes 4194320 | tf_op jit(solution)/shard_map/psum | solution.py:57
  492.0 5.8 %fusion.17 = f32[1,3,128,128]{3,1,2,0:T(4,128)S(1)} fusion(f32[64,128,128]{2,1,0:T(8,128)} %all-reduce.2.cloned.1.call-done, s32[64]{0:T(128)S(1)} %fusion.40, s32[3]{0:T(128)S(1)} %iota_add_fusion), kind=kOutput, calls=%fused_computation.24 | convolution fusion | flops 37748928 | bytes 4391180 | tf_op jit(solution)/shard_map/sk,kbc->sbc/dot_general | solution.py:60
  497.8 0.7 copy.66
  (8 shorter events, 0.0 us)
Async XLA Ops:
  6.5 39.3 %all-gather.3.cloned.1.call-start = ((), (), s32[]{:S(2)}) async-start(), calls=%async_computation | async-start | bytes 2359296 | tf_op jit(solution)/shard_map/all_gather | solution.py:26
  8.3 3.8 copy-start.3
  8.4 182.7 %all-gather.5.cloned.1.call-start = ((), (), s32[]{:S(2)}) async-start(), calls=%async_computation.1 | async-start | bytes 2129920 | tf_op jit(solution)/shard_map/all_gather | solution.py:30
  9.9 482.1 %all-reduce.2.cloned.1.call-start = ((), (), s32[]{:S(2)}) async-start(), calls=%async_computation.2 | async-start | bytes 8388608 | tf_op jit(solution)/shard_map/psum | solution.py:57
  11.5 2.3 copy-start.2
  191.0 1.9 copy-start
  192.9 1.2 copy-start.1
  205.5 0.7 copy-start.4
Sparse Core Ops, SparseCore 0:
  9.5 36.2 all-gather.2
  48.8 142.2 all-gather.4
  205.6 286.3 all-reduce.1
where the time goes:
time: 505 us
  waiting for transfers between devices  457 us (90%)
  matrix products  17 us (3%)
  between operations  13.3 us (3%)
  local copies, waits for them, and re-layouts  12.8 us (3%)
    psum x1, waiting for transfers between devices, local(): summed = lax.psum(block_grads, 'dp')  286 us
    all_gather x1, waiting for transfers between devices, local(): lax.all_gather(masters.astype(jnp.bfloat16), 'dp', axis=1, tiled=True)[0]  139 us
    all_gather x1, waiting for transfers between devices, local(): features = lax.all_gather(tokens, 'tensor', axis=1, tiled=True)  31.9 us
  transfers between devices with their start and end apart: 3, of which 3 were waited for; matrix products, arithmetic and copies ran while one was open for 2% of the time, Pallas kernels for 0%

commit v1 on v0

--- a/solution.py
+++ b/solution.py
@@ -2,6 +2,7 @@
 import jax.numpy as jnp
 from jax import lax
 from jax.sharding import PartitionSpec as P
+from jax.lax import axis_index, axis_size, ppermute
 
 
 def slot_index(owner_row, capacity):
@@ -23,7 +24,25 @@
 
 def local(tokens, hidden_grad, masters, block_row, block_col, owners):
     high = lax.Precision.HIGHEST
-    features = lax.all_gather(tokens, "tensor", axis=1, tiled=True)
+    piece_out, w_next, current_block = (axis_size("tensor"), axis_index("tensor"), tokens.shape[1])
+    bank = tuple(((ii, (ii + 1) % piece_out) for ii in range(piece_out)))
+    rack = tuple(((ii, (ii - 1) % piece_out) for ii in range(piece_out)))
+    features = jnp.zeros(
+        (*tokens.shape[:1], piece_out * current_block, *tokens.shape[2:]), tokens.dtype
+    )
+    features = lax.dynamic_update_slice_in_dim(features, tokens, w_next * current_block, axis=1)
+    plain = mid_arr = tokens
+    z2 = piece_out // 2
+    for idx in [*range(1, z2 + 1)]:
+        plain = ppermute(plain, "tensor", bank)
+        features = lax.dynamic_update_slice_in_dim(
+            features, plain, (w_next - idx) % piece_out * current_block, axis=1
+        )
+        if idx < piece_out - z2:
+            mid_arr = ppermute(mid_arr, "tensor", rack)
+            features = lax.dynamic_update_slice_in_dim(
+                features, mid_arr, (w_next + idx) % piece_out * current_block, axis=1
+            )
     token_count = features.shape[0]
     block_side = masters.shape[-1]
     kept_count = block_row.shape[1]

time: 505 us -> 470 us (0.931)
  waiting for transfers between devices: 457 us -> 405 us
  starting transfers between devices: 0.09 us -> 8.97 us
    all_gather x1 -> x0, waiting for transfers between devices: 31.9 us -> none  [local(): features = lax.all_gather(tokens, 'tensor', axis=1, tiled=True)]
    all_gather x1, waiting for transfers between devices: 139 us -> 111 us  [local(): lax.all_gather(masters.astype(jnp.bfloat16), 'dp', axis=1, tiled=True)[0]]
    ppermute x0 -> x7, starting transfers between devices: none -> 8.93 us  [the longest x3 8.9 us: local(): mid_arr = ppermute(mid_arr, 'tensor', rack)]
    ppermute x0 -> x7, waiting for transfers between devices: none -> 7.91 us  [the longest x4 7.9 us: local(): plain = ppermute(plain, 'tensor', bank)]
  transfers between devices with their start and end apart: 3 -> 9, of which waited for: 3 -> 5; matrix products, arithmetic and copies ran while one was open for 2% -> 4% of each run, Pallas kernels for 0% -> 0%
where the time goes in v1:
time: 470 us
  waiting for transfers between devices  405 us (86%)
  local copies, waits for them, and re-layouts  17.5 us (4%)
  matrix products  16.8 us (4%)
  between operations  13.7 us (3%)
  starting transfers between devices  8.97 us (2%)
  other arithmetic  8.02 us (2%)
    psum x1, waiting for transfers between devices, local(): summed = lax.psum(block_grads, 'dp')  286 us
    all_gather x1, waiting for transfers between devices, local(): lax.all_gather(masters.astype(jnp.bfloat16), 'dp', axis=1, tiled=True)[0]  111 us
  transfers between devices with their start and end apart: 9, of which 5 were waited for; matrix products, arithmetic and copies ran while one was open for 4% of the time, Pallas kernels for 0%

profile of v1, /device:TPU:8, one launch (start us, length us, event | category | flops | bytes accessed | tf_op | source)
XLA Modules:
  0.0 469.9 jit_solution(285779372876205175)
XLA Ops:
  6.5 1.5 bitcast_convert_fusion
  8.1 0.0 all-gather.2.cloned.1.call-update
  8.1 0.0 all-reduce.2.cloned.1.call-start
  8.2 1.1 copy.52
  9.3 0.0 collective-permute-start
  9.3 1.7 collective-permute-start.1
  11.0 0.7 fusion.38
  11.7 0.7 compare_and_fusion.1
  12.4 0.7 fusion.39
  13.0 1.2 compare_and_fusion
  14.2 1.0 collective-permute-done
  15.2 0.0 collective-permute-start.2
  15.2 0.3 broadcast_in_dim.29
  15.5 0.0 collective-permute-done.1
  15.6 3.2 collective-permute-start.3
  18.8 1.3 copy.57
  20.1 1.6 copy.58
  21.7 1.7 gather_fusion.1
  23.4 0.0 collective-permute-done.2
  23.4 0.0 collective-permute-start.4
  23.4 1.0 constant_dynamic-update-slice_fusion.6
  24.4 0.0 collective-permute-done.3
  24.4 3.9 collective-permute-start.5
  28.4 1.0 constant_dynamic-update-slice_fusion.4
  29.4 2.2 collective-permute-done.4
  31.6 1.0 constant_dynamic-update-slice_fusion.3
  32.7 4.7 collective-permute-done.6
  37.4 2.9 copy.55
  40.3 2.3 gather_fusion
  42.6 0.6 fusion.24
  43.3 1.2 copy.67
  44.5 111.2 %all-gather.2.cloned.1.call-done = bf16[1,64,128,128]{3,2,0,1:T(8,128)(2,1)} async-done(((bf16[1,1,128,128]{3,2,0,1:T(8,128)(2,1)}), bf16[1,64,128,128]{3,2,0,1:T(8,128)(2,1)}) %all-gather.2.cloned.1.call-update) | async-done | bytes 2097168 | tf_op jit(solution)/shard_map/all_gather | solution.py:49
  155.6 1.9 convolution_bitcast_fusion
  157.5 0.0 copy-done
  157.6 0.0 copy-start.3
  157.6 0.5 convolution_bitcast_fusion.1
  158.1 0.7 copy-done.1
  158.8 3.4 fusion.9
  162.2 3.7 fusion.7
  165.9 0.8 fusion.22
  166.7 0.8 fusion.20
  167.4 2.5 pad_maximum_fusion
  169.9 0.0 all-reduce.2.cloned.1.call-update
  169.9 0.6 copy-done.4
  170.6 0.2 convert_reduce_fusion
  170.7 285.9 %all-reduce.2.cloned.1.call-done = f32[64,128,128]{2,1,0:T(8,128)} async-done(((f32[64,128,128]{2,1,0:T(8,128)}), f32[64,128,128]{2,1,0:T(8,128)}) %all-reduce.2.cloned.1.call-update) | async-done | bytes 4194320 | tf_op jit(solution)/shard_map/psum | solution.py:76
  456.6 5.8 %fusion.17 = f32[1,3,128,128]{3,1,2,0:T(4,128)S(1)} fusion(f32[64,128,128]{2,1,0:T(8,128)} %all-reduce.2.cloned.1.call-done, s32[64]{0:T(128)S(1)} %fusion.40, s32[3]{0:T(128)S(1)} %iota_add_fusion), kind=kOutput, calls=%fused_computation.24 | convolution fusion | flops 37748928 | bytes 4391180 | tf_op jit(solution)/shard_map/sk,kbc->sbc/dot_general | solution.py:79
  462.4 0.7 copy.72
  (20 shorter events, 0.2 us)
Async XLA Ops:
  6.5 12.3 %copy-start.2 = (bf16[128,3584]{1,0:T(8,128)(2,1)S(1)}, bf16[128,3584]{1,0:T(8,128)(2,1)}, u32[]{:S(2)}) copy-start(bf16[128,3584]{1,0:T(8,128)(2,1)} %param.7) | copy-start | bytes 2752516
  6.5 149.1 %all-gather.2.cloned.1.call-start = ((), (), s32[]{:S(2)}) async-start(), calls=%async_computation | async-start | bytes 2129920 | tf_op jit(solution)/shard_map/all_gather | solution.py:49
  8.1 448.5 %all-reduce.2.cloned.1.call-start = ((), (), s32[]{:S(2)}) async-start(), calls=%async_computation.1 | async-start | bytes 8388608 | tf_op jit(solution)/shard_map/psum | solution.py:76
  9.3 5.9 %collective-permute-start = (bf16[128,1024]{0,1:T(8,128)(2,1)S(1)}, bf16[128,1024]{0,1:T(8,128)(2,1)}, u32[]{:S(2)}, u32[]{:S(2)}) collective-permute-start(bf16[128,1024]{0,1:T(8,128)(2,1)S(1)} %copy.52), channel_id=1, source_target_pairs={{0,1},{1,2},{2,3},{3,4},{4,5},{5,6},{6,7},{7,0},{8,9},{9,10},{10,1... | collective-permute-start | bytes 786440 | tf_op jit(solution)/shard_map/ppermute | solution.py:37
  9.3 6.2 %collective-permute-start.1 = (bf16[128,1024]{0,1:T(8,128)(2,1)S(1)}, bf16[128,1024]{0,1:T(8,128)(2,1)S(1)}, u32[]{:S(2)}, u32[]{:S(2)}) collective-permute-start(bf16[128,1024]{0,1:T(8,128)(2,1)S(1)} %copy.52), channel_id=1, source_target_pairs={{0,7},{1,0},{2,1},{3,2},{4,3},{5,4},{6,5},{7,6},{8,15},{9,8},{10,9... | collective-permute-start | bytes 786440 | tf_op jit(solution)/shard_map/ppermute | solution.py:42
  15.2 8.2 %collective-permute-start.2 = (bf16[128,1024]{0,1:T(8,128)(2,1)}, bf16[128,1024]{0,1:T(8,128)(2,1)}, u32[]{:S(2)}, u32[]{:S(2)}) collective-permute-start(bf16[128,1024]{0,1:T(8,128)(2,1)} %collective-permute-done), channel_id=1, source_target_pairs={{0,1},{1,2},{2,3},{3,4},{4,5},{5,6},{6,7},{7,0},{8,9},{9,10},{10,1... | collective-permute-start | bytes 786440 | tf_op jit(solution)/shard_map/ppermute | solution.py:37
  15.6 8.9 %collective-permute-start.3 = (bf16[128,1024]{0,1:T(8,128)(2,1)S(1)}, bf16[128,1024]{0,1:T(8,128)(2,1)}, u32[]{:S(2)}, u32[]{:S(2)}) collective-permute-start(bf16[128,1024]{0,1:T(8,128)(2,1)S(1)} %collective-permute-done.1), channel_id=1, source_target_pairs={{0,7},{1,0},{2,1},{3,2},{4,3},{5,4},{6,5},{7,6},{8,15},{9,8},{10,9... | collective-permute-start | bytes 786440 | tf_op jit(solution)/shard_map/ppermute | solution.py:42
  23.4 8.2 %collective-permute-start.4 = (bf16[128,1024]{0,1:T(8,128)(2,1)}, bf16[128,1024]{0,1:T(8,128)(2,1)S(1)}, u32[]{:S(2)}, u32[]{:S(2)}) collective-permute-start(bf16[128,1024]{0,1:T(8,128)(2,1)} %collective-permute-done.2), channel_id=1, source_target_pairs={{0,1},{1,2},{2,3},{3,4},{4,5},{5,6},{6,7},{7,0},{8,9},{9,10},{10,1... | collective-permute-start | bytes 786440 | tf_op jit(solution)/shard_map/ppermute | solution.py:37
  24.4 8.2 %collective-permute-start.5 = (bf16[128,1024]{0,1:T(8,128)(2,1)}, bf16[128,1024]{0,1:T(8,128)(2,1)S(1)}, u32[]{:S(2)}, u32[]{:S(2)}) collective-permute-start(bf16[128,1024]{0,1:T(8,128)(2,1)} %collective-permute-done.3), channel_id=1, source_target_pairs={{0,7},{1,0},{2,1},{3,2},{4,3},{5,4},{6,5},{7,6},{8,15},{9,8},{10,9... | collective-permute-start | bytes 786440 | tf_op jit(solution)/shard_map/ppermute | solution.py:42
  31.6 5.8 %collective-permute-start.6 = (bf16[128,1024]{0,1:T(8,128)(2,1)S(1)}, bf16[128,1024]{0,1:T(8,128)(2,1)S(1)}, u32[]{:S(2)}, u32[]{:S(2)}) collective-permute-start(bf16[128,1024]{0,1:T(8,128)(2,1)S(1)} %collective-permute-done.4), channel_id=1, source_target_pairs={{0,1},{1,2},{2,3},{3,4},{4,5},{5,6},{6,7},{7,0},{8,9},{9,10},{10,1... | collective-permute-start | bytes 786440 | tf_op jit(solution)/shard_map/ppermute | solution.py:37
  155.6 1.9 copy-start
  157.5 1.2 copy-start.1
  157.6 1.2 copy-start.3
  157.6 1.2 copy-start.5
  169.9 0.7 copy-start.4
Sparse Core Ops, SparseCore 0:
  10.3 145.2 all-gather.1
  170.1 286.4 all-reduce.1
